TPU v7x, 512 devices: a whole 4x4x16 slice. The times are simulated.
512 devices in a mesh: span: 64 (over z_lo, x, core), chord: 8 (over z_hi, y).
Axes of the slice: x: 4, y: 4, z: 16 (z_hi: 2, z_lo: 8; z = z_hi * 8 + z_lo), core: 2. Of those that a mesh axis runs over, the one named last changes fastest.
Arguments:
- adjoint_flow: float32 [5, 16, 512, 1024], P(None, None, 'span', 'chord'), may hold values from -6 to 6
- flow_grad: float32 [5, 16, 512, 1024], P(None, None, 'span', 'chord'), may hold values from -6 to 6
- diagonal: float32 [16, 512, 1024], P(None, 'span', 'chord'), may hold values from 4 to 6
- couplings: float32 [3, 16, 512, 1024], P(None, None, 'span', 'chord'), may hold values from 0.3 to 1.5
- upwind: float32 [3, 5, 5], replicated, may hold values from -2.5 to 2.5
- downwind: float32 [3, 5, 5], replicated, may hold values from -2.5 to 2.5
- pressure_row: float32 [5], replicated, may hold values from -4 to 4
- face_normal: float32 [3, 512, 1024], P(None, 'span', 'chord'), may hold values from -6 to 6
- face_node: int32 [512, 1024], P('span', 'chord'), may hold values from 0 to 65535, as said below
- face_count: int32 [64, 8], P('span', 'chord'), may hold values from 128 to 1024, as said below
- adjoint_shell: float32 [6, 65536], P(None, 'span'), may hold values from -6 to 6
- shell_grad: float32 [6, 65536], P(None, 'span'), may hold values from -6 to 6
- node_precond: float32 [6, 6, 65536], P(None, None, 'span'), as said below
- element_stiffness: float32 [24, 24, 65536], P(None, None, ('span', 'chord')), as said below
- connectivity: int32 [4, 65536], P(None, ('span', 'chord')), may hold values from 0 to 65535, as said below
Outputs:
- flow_adjoint: float32 [5, 16, 512, 1024], P(None, None, 'span', 'chord')
- shell_adjoint: float32 [6, 65536], P(None, 'span')
Inputs may be any that keep to these rules, and one draw needn't show every extreme that they name: `face_node`: a wall face in the span cells of span index s names a node from max(s - 1, 0) * 1024 to min(s + 2, 64) * 1024 - 1. `face_count`: on each device the wall faces in use are the first ones in span-major, chord-minor order. `connectivity`: the elements of span index s use nodes from s * 1024 to min((s + 1) * 1024 + 64, 65536) - 1. `node_precond`: each node block is near 0.15 times the identity. `element_stiffness`: each element block is symmetric and near the identity.
All inputs are finite; a program needn't handle non-finite values.
Results may differ from a plain program's by a relative error of at most 0.00013.
Values sent between devices are 32-bit elements; how exact they have to be, the bound alone decides.
No kernel may reach another device: no remote copies, remote signals or barrier semaphores. Data moves between devices by JAX's collectives and lax.ppermute only.
A program may use at most 64 MiB of HBM per device.

v0:
```python
import jax
import jax.numpy as jnp
from jax import lax
from jax.sharding import PartitionSpec as P

NB = 64
SW = 4
SS = 3


def shifted(value, axis, steps):
    count = lax.axis_size(axis)
    initial, last = (max(0, -steps), min(count, count - steps))
    return lax.ppermute(value, axis, [(source, source + steps) for source in range(initial, last)])


def with_halo(cells, sides, width):
    for axis, dim in sides:
        count = lax.axis_size(axis)
        ends = count - 1
        head = lax.slice_in_dim(cells, 0, width, axis=dim)
        tail = lax.slice_in_dim(cells, cells.shape[dim] - width, cells.shape[dim], axis=dim)
        cells = jnp.concatenate(
            [
                lax.ppermute(tail, axis, [(i, (i + 1) % count) for i in range(ends)]),
                cells,
                lax.ppermute(head, axis, [((i + 1) % count, i) for i in range(ends)]),
            ],
            axis=dim,
        )
    return cells


def relax_cells(state, inv_diag, couplings, source, upwind, downwind):
    centre = state[:, :, 1:-1, 1:-1]
    normal_pad = jnp.pad(centre, ((0, 0), (1, 1), (0, 0), (0, 0)))
    pairs = (
        (normal_pad[:, 2:], normal_pad[:, :-2]),
        (state[:, :, 2:, 1:-1], state[:, :, :-2, 1:-1]),
        (state[:, :, 1:-1, 2:], state[:, :, 1:-1, :-2]),
    )
    neighbours = jnp.zeros_like(source)
    for direction in range(3):
        forward, backward = pairs[direction]
        flux_term = jnp.einsum(
            "ij,jnsc->insc", upwind[direction], forward, precision=lax.Precision.HIGHEST
        )
        flux_term = flux_term + jnp.einsum(
            "ij,jnsc->insc", downwind[direction], backward, precision=lax.Precision.HIGHEST
        )
        neighbours = neighbours + couplings[direction][None] * flux_term
    return inv_diag[None] * (source + neighbours)


def spread(partial_value, node_dev):
    own_block = partial_value[:, node_dev : 2 * node_dev]
    from_lower = shifted(partial_value[:, 2 * node_dev :], "span", 1)
    from_upper = shifted(partial_value[:, :node_dev], "span", -1)
    return own_block + from_lower + from_upper


def element_terms(field, element_stiffness, local_nodes):
    node_dev = field.shape[1]
    count_elems = local_nodes.shape[1]
    rim_nodes = shifted(field[:, :NB], "span", -1)
    extended = jnp.concatenate([field, rim_nodes], axis=1)
    element_values = extended[:, local_nodes]
    element_values = jnp.transpose(element_values, (1, 0, 2)).reshape(24, count_elems)
    element_forces = jnp.einsum(
        "ije,je->ie", element_stiffness, element_values, precision=lax.Precision.HIGHEST
    )
    element_forces = jnp.transpose(element_forces.reshape(4, 6, count_elems), (1, 0, 2)).reshape(
        6, 4 * count_elems
    )
    assembled = jax.ops.segment_sum(element_forces.T, local_nodes.reshape(-1), node_dev + NB).T
    spill = shifted(assembled[:, node_dev:], "span", 1)
    return assembled[:, :node_dev].at[:, :NB].add(spill)


def per_device(
    adjoint_flow,
    flow_grad,
    diagonal,
    couplings,
    upwind,
    downwind,
    pressure_row,
    face_normal,
    face_node,
    face_count,
    adjoint_shell,
    shell_grad,
    node_precond,
    element_stiffness,
    connectivity,
):
    span_at = lax.axis_index("span")
    node_dev = adjoint_shell.shape[1]
    wall_layer = adjoint_flow[:, 0]
    span_cells = wall_layer.shape[1]
    chord_cells = wall_layer.shape[2]
    local_index = (
        jnp.arange(span_cells, dtype=jnp.int32)[:, None] * chord_cells
        + jnp.arange(chord_cells, dtype=jnp.int32)[None, :]
    )
    active = (local_index < face_count[0, 0]).astype(jnp.float32)
    pressure = (
        jnp.einsum("j,jsc->sc", pressure_row, wall_layer, precision=lax.Precision.HIGHEST) * active
    )
    loads_face = face_normal * pressure[None]
    reach_index = face_node - (span_at - 1) * node_dev
    partial_value = jax.ops.segment_sum(
        loads_face.reshape(3, -1).T, reach_index.reshape(-1), 3 * node_dev
    ).T
    partial_value = lax.psum(partial_value, "chord")
    node_load = spread(partial_value, node_dev)
    load_full = jnp.concatenate([node_load, jnp.zeros((3, node_dev), jnp.float32)], axis=0)
    local_nodes = connectivity - span_at * node_dev
    shell_state = adjoint_shell
    for turn_index in range(SS):
        local_forces = element_terms(shell_state, element_stiffness, local_nodes)
        stiff_total = lax.psum(local_forces, "chord")
        residual = shell_grad - load_full - stiff_total
        shell_state = shell_state + jnp.einsum(
            "ijn,jn->in", node_precond, residual, precision=lax.Precision.HIGHEST
        )
    reach = with_halo(shell_state[:3], (("span", 1),), node_dev)
    picked = reach[:, reach_index]
    disp = jnp.einsum("isc,isc->sc", face_normal, picked, precision=lax.Precision.HIGHEST) * active
    source = flow_grad.at[:, 0].add(-pressure_row[:, None, None] * disp[None])
    inv_diag = 1.0 / diagonal
    state = adjoint_flow
    for turn_index in range(SW):
        padded = with_halo(state, (("span", 2), ("chord", 3)), 1)
        state = relax_cells(padded, inv_diag, couplings, source, upwind, downwind)
    return (state, shell_state)


def solution(mesh):
    return jax.shard_map(
        per_device,
        mesh=mesh,
        in_specs=(
            P(None, None, "span", "chord"),
            P(None, None, "span", "chord"),
            P(None, "span", "chord"),
            P(None, None, "span", "chord"),
            P(),
            P(),
            P(),
            P(None, "span", "chord"),
            P("span", "chord"),
            P("span", "chord"),
            P(None, "span"),
            P(None, "span"),
            P(None, None, "span"),
            P(None, None, ("span", "chord")),
            P(None, ("span", "chord")),
        ),
        out_specs=(P(None, None, "span", "chord"), P(None, "span")),
        check_vma=False,
    )
```

profile of v0, /device:TPU:223, one launch (start us, length us, event | category | flops | bytes accessed | tf_op | source)
XLA Modules:
  0.0 633.0 jit_solution(17247283147842668898)
XLA Ops:
  1.4 2.6 collective-permute-start.2
  5.8 5.1 collective-permute-start.11
  19.8 2.4 scatter_custom_fusion.1
  22.8 5.7 collective-permute-start.3
  28.8 6.4 %scatter_custom_fusion = f32[3072,3]{1,0:T(8,128)S(1)} fusion(s32[1024]{0:T(1024)S(1)} %subtract_bitcast_fusion.3, f32[1024,3]{1,0:T(8,128)S(1)} %bitcast.192, f32[]{:T(128)} %constant.114.clone.1), kind=kCustom, calls=%fused_computation.52 | custom fusion | flops 3072 | bytes 36868 | tf_op jit(solution)/shard_map/scatter-add | solution.py:112
  36.7 194.2 %all-reduce.5 = (f32[6,1024]{0,1:T(8,128)}, f32[3,3072]{0,1:T(8,128)}) all-reduce(f32[6,1024]{0,1:T(8,128)S(1)} %fusion.84, f32[3,3072]{0,1:T(8,128)S(1)} %bitcast.181), channel_id=1, replica_groups=mesh['span'=64,'chord'=8] {'chord'}, use_global_device_ids=true, to_apply=%region_4.0 | all-reduce | flops 15360 | bytes 122880 | tf_op jit(solution)/shard_map/psum | solution.py:122
  234.9 18.2 %collective-permute-start.1 = (f32[3,1024]{0,1:T(8,128)S(1)}, f32[3,1024]{0,1:T(8,128)}, u32[]{:S(2)}, u32[]{:S(2)}) collective-permute-start(f32[3,1024]{0,1:T(8,128)S(1)} %get-tuple-element.61), channel_id=1, source_target_pairs={{8,0},{16,8},{24,16},{32,24},{40,32},{48,40},{56,48},{64,56},{72,6... | collective-permute-start | bytes 36872 | tf_op jit(solution)/shard_map/ppermute | solution.py:14
  257.1 8.7 %collective-permute-start.4 = (f32[6,64]{1,0:T(8,128)S(1)}, f32[6,64]{1,0:T(8,128)S(1)}, u32[]{:S(2)}, u32[]{:S(2)}) collective-permute-start(f32[6,64]{1,0:T(8,128)S(1)} %slice.401), channel_id=1, source_target_pairs={{8,0},{16,8},{24,16},{32,24},{40,32},{48,40},{56,48},{64,56},{72,6... | collective-permute-start | bytes 4616 | tf_op jit(solution)/shard_map/ppermute | solution.py:14
  271.4 2.8 scatter_custom_fusion.2
  280.1 68.6 %psum.30 = f32[6,1024]{0,1:T(8,128)S(1)} all-reduce(f32[6,1024]{0,1:T(8,128)} %fusion.85), channel_id=1, replica_groups=mesh['span'=64,'chord'=8] {'chord'}, use_global_device_ids=true, to_apply=%region_6.0 | all-reduce | flops 6144 | bytes 49152 | tf_op jit(solution)/shard_map/psum | solution.py:122
  350.9 19.7 %collective-permute-start.6 = (f32[6,64]{1,0:T(8,128)S(1)}, f32[6,64]{1,0:T(8,128)S(1)}, u32[]{:S(2)}, u32[]{:S(2)}) collective-permute-start(f32[6,64]{1,0:T(8,128)S(1)} %slice.405), channel_id=1, source_target_pairs={{8,0},{16,8},{24,16},{32,24},{40,32},{48,40},{56,48},{64,56},{72,6... | collective-permute-start | bytes 4616 | tf_op jit(solution)/shard_map/ppermute | solution.py:14
  370.6 2.2 fusion.3
  374.5 2.5 scatter_custom_fusion.3
  380.8 78.4 %psum.31 = f32[6,1024]{0,1:T(8,128)S(1)} all-reduce(f32[6,1024]{0,1:T(8,128)S(1)} %fusion.86), channel_id=1, replica_groups=mesh['span'=64,'chord'=8] {'chord'}, use_global_device_ids=true, to_apply=%region_8.0 | all-reduce | flops 6144 | bytes 49152 | tf_op jit(solution)/shard_map/psum | solution.py:122
  460.2 13.6 %collective-permute-start.8 = (f32[3,1024]{1,0:T(4,128)S(1)}, f32[3,1024]{1,0:T(4,128)S(1)}, u32[]{:S(2)}, u32[]{:S(2)}) collective-permute-start(f32[3,1024]{1,0:T(4,128)S(1)} %slice.409), channel_id=1, source_target_pairs={{0,8},{8,16},{16,24},{24,32},{32,40},{40,48},{48,56},{56,64},{64,7... | collective-permute-start | bytes 36872 | tf_op jit(solution)/shard_map/ppermute | solution.py:25
  477.0 4.0 collective-permute-done.9
  481.5 4.0 gather_fusion.3
  489.5 14.8 %collective-permute-start.13 = (f32[5,16,10,1]{1,3,2,0:T(1,128)S(1)}, f32[5,16,10,1]{1,3,2,0:T(1,128)S(1)}, u32[]{:S(2)}, u32[]{:S(2)}) collective-permute-start(f32[5,16,10,1]{1,3,2,0:T(1,128)S(1)} %copy.116), channel_id=1, source_target_pairs={{0,1},{1,2},{2,3},{3,4},{4,5},{5,6},{6,7},{8,9},{9,10},{10,11},{11... | collective-permute-start | bytes 9608 | tf_op jit(solution)/shard_map/ppermute | solution.py:25
  510.7 9.3 %collective-permute-done.12 = f32[5,16,10,1]{1,3,2,0:T(1,128)S(1)} collective-permute-done((f32[5,16,10,1]{1,3,2,0:T(1,128)S(1)}, f32[5,16,10,1]{1,3,2,0:T(1,128)S(1)}, u32[]{:S(2)}, u32[]{:S(2)}) %collective-permute-start.12) | collective-permute-done | bytes 3232 | tf_op jit(solution)/shard_map/ppermute | solution.py:27
  524.7 3.5 collective-permute-start.15
  530.8 5.1 collective-permute-done.14
  536.9 3.9 collective-permute-start.17
  547.2 10.3 %collective-permute-done.16 = f32[5,16,10,1]{1,3,2,0:T(1,128)} collective-permute-done((f32[5,16,10,1]{1,3,2,0:T(1,128)}, f32[5,16,10,1]{1,3,2,0:T(1,128)}, u32[]{:S(2)}, u32[]{:S(2)}) %collective-permute-start.16) | collective-permute-done | bytes 3232 | tf_op jit(solution)/shard_map/ppermute | solution.py:27
  561.7 3.3 collective-permute-start.19
  567.5 5.2 collective-permute-done.18
  574.0 3.1 collective-permute-start.21
  578.1 2.3 collective-permute-start.20
  583.0 10.8 %collective-permute-done.20 = f32[5,16,10,1]{1,3,2,0:T(1,128)} collective-permute-done((f32[5,16,10,1]{1,3,2,0:T(1,128)}, f32[5,16,10,1]{1,3,2,0:T(1,128)}, u32[]{:S(2)}, u32[]{:S(2)}) %collective-permute-start.20) | collective-permute-done | bytes 3232 | tf_op jit(solution)/shard_map/ppermute | solution.py:27
  598.1 3.3 collective-permute-start.23
  603.9 5.4 collective-permute-done.22
  613.6 3.6 collective-permute-start.24
  618.9 10.4 %collective-permute-done.24 = f32[5,16,10,1]{1,3,2,0:T(1,128)} collective-permute-done((f32[5,16,10,1]{1,3,2,0:T(1,128)}, f32[5,16,10,1]{1,3,2,0:T(1,128)}, u32[]{:S(2)}, u32[]{:S(2)}) %collective-permute-start.24) | collective-permute-done | bytes 3232 | tf_op jit(solution)/shard_map/ppermute | solution.py:27
  (245 shorter events, 96.7 us)
Async XLA Ops:
  1.4 16.0 %collective-permute-start.2 = (f32[6,64]{1,0:T(8,128)S(1)}, f32[6,64]{1,0:T(8,128)S(1)}, u32[]{:S(2)}, u32[]{:S(2)}) collective-permute-start(f32[6,64]{1,0:T(8,128)S(1)} %slice.324), channel_id=1, source_target_pairs={{8,0},{16,8},{24,16},{32,24},{40,32},{48,40},{56,48},{64,56},{72,6... | collective-permute-start | bytes 4616 | tf_op jit(solution)/shard_map/ppermute | solution.py:14
  5.1 23.4 %copy-start.37 = (s32[8,128]{1,0:T(8,128)S(1)}, s32[8,128]{1,0:T(8,128)}, u32[]{:S(2)}) copy-start(s32[8,128]{1,0:T(8,128)} %param.31) | copy-start | bytes 12292
  5.8 481.1 %collective-permute-start.11 = (f32[5,16,1,128]{3,0,2,1:T(8,128)}, f32[5,16,1,128]{3,0,2,1:T(8,128)}, u32[]{:S(2)}, u32[]{:S(2)}) collective-permute-start(f32[5,16,1,128]{3,0,2,1:T(8,128)} %get-tuple-element.77), channel_id=1, source_target_pairs={{0,8},{8,16},{16,24},{24,32},{32,40},{40,48},{48,56},{56,64},{64,7... | collective-permute-start | bytes 122888 | tf_op jit(solution)/shard_map/ppermute | solution.py:25
  10.9 477.1 %collective-permute-start.10 = (f32[5,16,1,128]{3,0,2,1:T(8,128)}, f32[5,16,1,128]{3,0,2,1:T(8,128)}, u32[]{:S(2)}, u32[]{:S(2)}) collective-permute-start(f32[5,16,1,128]{3,0,2,1:T(8,128)} %get-tuple-element.76), channel_id=1, source_target_pairs={{8,0},{16,8},{24,16},{32,24},{40,32},{48,40},{56,48},{64,56},{72,6... | collective-permute-start | bytes 122888 | tf_op jit(solution)/shard_map/ppermute | solution.py:27
  12.8 22.4 %copy-start.39 = (s32[8]{0:T(128)}, s32[8]{0:T(128)S(1)}, u32[]{:S(2)}) copy-start(s32[8]{0:T(128)S(1)} %iota_multiply_fusion) | copy-start | bytes 100
  22.8 13.2 %collective-permute-start.3 = (f32[6,64]{0,1:T(8,128)}, f32[6,64]{0,1:T(8,128)S(1)}, u32[]{:S(2)}, u32[]{:S(2)}) collective-permute-start(f32[6,64]{0,1:T(8,128)} %slice.400), channel_id=1, source_target_pairs={{0,8},{8,16},{16,24},{24,32},{32,40},{40,48},{48,56},{56,64},{64,7... | collective-permute-start | bytes 4616 | tf_op jit(solution)/shard_map/ppermute | solution.py:14
  230.9 22.2 %copy-start = (f32[5,16,8,128]{3,2,1,0:T(8,128)S(1)}, f32[5,16,8,128]{3,2,1,0:T(8,128)}, u32[]{:S(2)}) copy-start(f32[5,16,8,128]{3,2,1,0:T(8,128)} %param.23) | copy-start | bytes 983044
  230.9 22.8 %copy-start.34 = (f32[6,1024]{1,0:T(8,128)S(1)}, f32[6,1024]{1,0:T(8,128)}, u32[]{:S(2)}) copy-start(f32[6,1024]{1,0:T(8,128)} %param.34) | copy-start | bytes 73732
  233.0 21.0 %collective-permute-start = (f32[3,1024]{0,1:T(8,128)}, f32[3,1024]{0,1:T(8,128)S(1)}, u32[]{:S(2)}, u32[]{:S(2)}) collective-permute-start(f32[3,1024]{0,1:T(8,128)} %get-tuple-element.60), channel_id=1, source_target_pairs={{0,8},{8,16},{16,24},{24,32},{32,40},{40,48},{48,56},{56,64},{64,7... | collective-permute-start | bytes 36872 | tf_op jit(solution)/shard_map/ppermute | solution.py:14
  234.9 19.8 %collective-permute-start.1 = (f32[3,1024]{0,1:T(8,128)S(1)}, f32[3,1024]{0,1:T(8,128)}, u32[]{:S(2)}, u32[]{:S(2)}) collective-permute-start(f32[3,1024]{0,1:T(8,128)S(1)} %get-tuple-element.61), channel_id=1, source_target_pairs={{8,0},{16,8},{24,16},{32,24},{40,32},{48,40},{56,48},{64,56},{72,6... | collective-permute-start | bytes 36872 | tf_op jit(solution)/shard_map/ppermute | solution.py:14
  257.1 10.3 %collective-permute-start.4 = (f32[6,64]{1,0:T(8,128)S(1)}, f32[6,64]{1,0:T(8,128)S(1)}, u32[]{:S(2)}, u32[]{:S(2)}) collective-permute-start(f32[6,64]{1,0:T(8,128)S(1)} %slice.401), channel_id=1, source_target_pairs={{8,0},{16,8},{24,16},{32,24},{40,32},{48,40},{56,48},{64,56},{72,6... | collective-permute-start | bytes 4616 | tf_op jit(solution)/shard_map/ppermute | solution.py:14
  274.2 4.6 collective-permute-start.5
  349.6 23.6 %copy-start.36 = (s32[1024]{0:T(1024)S(1)}, s32[1024]{0:T(1024)}, u32[]{:S(2)}) copy-start(s32[1024]{0:T(1024)} %copy-done.35) | copy-start | bytes 12292
  350.9 22.0 %collective-permute-start.6 = (f32[6,64]{1,0:T(8,128)S(1)}, f32[6,64]{1,0:T(8,128)S(1)}, u32[]{:S(2)}, u32[]{:S(2)}) collective-permute-start(f32[6,64]{1,0:T(8,128)S(1)} %slice.405), channel_id=1, source_target_pairs={{8,0},{16,8},{24,16},{32,24},{40,32},{48,40},{56,48},{64,56},{72,6... | collective-permute-start | bytes 4616 | tf_op jit(solution)/shard_map/ppermute | solution.py:14
  377.0 3.1 collective-permute-start.7
  460.2 26.6 %copy-start.31 = (f32[6,1024]{1,0:T(8,128)}, f32[6,1024]{1,0:T(8,128)S(1)}, u32[]{:S(2)}) copy-start(f32[6,1024]{1,0:T(8,128)S(1)} %bitcast_add_fusion) | copy-start | bytes 73732
  460.2 16.8 %collective-permute-start.8 = (f32[3,1024]{1,0:T(4,128)S(1)}, f32[3,1024]{1,0:T(4,128)S(1)}, u32[]{:S(2)}, u32[]{:S(2)}) collective-permute-start(f32[3,1024]{1,0:T(4,128)S(1)} %slice.409), channel_id=1, source_target_pairs={{0,8},{8,16},{16,24},{24,32},{32,40},{40,48},{48,56},{56,64},{64,7... | collective-permute-start | bytes 36872 | tf_op jit(solution)/shard_map/ppermute | solution.py:25
  473.8 7.2 %collective-permute-start.9 = (f32[3,1024]{1,0:T(4,128)S(1)}, f32[3,1024]{1,0:T(4,128)S(1)}, u32[]{:S(2)}, u32[]{:S(2)}) collective-permute-start(f32[3,1024]{1,0:T(4,128)S(1)} %slice.409), channel_id=1, source_target_pairs={{8,0},{16,8},{24,16},{32,24},{40,32},{48,40},{56,48},{64,56},{72,6... | collective-permute-start | bytes 36872 | tf_op jit(solution)/shard_map/ppermute | solution.py:27
  489.5 19.3 %collective-permute-start.13 = (f32[5,16,10,1]{1,3,2,0:T(1,128)S(1)}, f32[5,16,10,1]{1,3,2,0:T(1,128)S(1)}, u32[]{:S(2)}, u32[]{:S(2)}) collective-permute-start(f32[5,16,10,1]{1,3,2,0:T(1,128)S(1)} %copy.116), channel_id=1, source_target_pairs={{0,1},{1,2},{2,3},{3,4},{4,5},{5,6},{6,7},{8,9},{9,10},{10,11},{11... | collective-permute-start | bytes 9608 | tf_op jit(solution)/shard_map/ppermute | solution.py:25
  504.6 15.4 %collective-permute-start.12 = (f32[5,16,10,1]{1,3,2,0:T(1,128)S(1)}, f32[5,16,10,1]{1,3,2,0:T(1,128)S(1)}, u32[]{:S(2)}, u32[]{:S(2)}) collective-permute-start(f32[5,16,10,1]{1,3,2,0:T(1,128)S(1)} %copy.113), channel_id=1, source_target_pairs={{1,0},{2,1},{3,2},{4,3},{5,4},{6,5},{7,6},{9,8},{10,9},{11,10},{12... | collective-permute-start | bytes 9608 | tf_op jit(solution)/shard_map/ppermute | solution.py:27
  524.7 6.0 collective-permute-start.15
  528.2 7.7 %collective-permute-start.14 = (f32[5,16,1,128]{3,0,2,1:T(8,128)S(1)}, f32[5,16,1,128]{3,0,2,1:T(8,128)S(1)}, u32[]{:S(2)}, u32[]{:S(2)}) collective-permute-start(f32[5,16,1,128]{3,0,2,1:T(8,128)S(1)} %get-tuple-element.75), channel_id=1, source_target_pairs={{8,0},{16,8},{24,16},{32,24},{40,32},{48,40},{56,48},{64,56},{72,6... | collective-permute-start | bytes 122888 | tf_op jit(solution)/shard_map/ppermute | solution.py:27
  536.9 7.6 %collective-permute-start.17 = (f32[5,16,10,1]{1,3,2,0:T(1,128)S(1)}, f32[5,16,10,1]{1,3,2,0:T(1,128)}, u32[]{:S(2)}, u32[]{:S(2)}) collective-permute-start(f32[5,16,10,1]{1,3,2,0:T(1,128)S(1)} %copy.121), channel_id=1, source_target_pairs={{0,1},{1,2},{2,3},{3,4},{4,5},{5,6},{6,7},{8,9},{9,10},{10,11},{11... | collective-permute-start | bytes 9608 | tf_op jit(solution)/shard_map/ppermute | solution.py:25
  541.8 15.7 %collective-permute-start.16 = (f32[5,16,10,1]{1,3,2,0:T(1,128)}, f32[5,16,10,1]{1,3,2,0:T(1,128)}, u32[]{:S(2)}, u32[]{:S(2)}) collective-permute-start(f32[5,16,10,1]{1,3,2,0:T(1,128)} %copy.119), channel_id=1, source_target_pairs={{1,0},{2,1},{3,2},{4,3},{5,4},{6,5},{7,6},{9,8},{10,9},{11,10},{12... | collective-permute-start | bytes 9608 | tf_op jit(solution)/shard_map/ppermute | solution.py:27
  561.7 5.8 collective-permute-start.19
  565.0 7.7 %collective-permute-start.18 = (f32[5,16,1,128]{3,0,2,1:T(8,128)S(1)}, f32[5,16,1,128]{3,0,2,1:T(8,128)S(1)}, u32[]{:S(2)}, u32[]{:S(2)}) collective-permute-start(f32[5,16,1,128]{3,0,2,1:T(8,128)S(1)} %get-tuple-element.73), channel_id=1, source_target_pairs={{8,0},{16,8},{24,16},{32,24},{40,32},{48,40},{56,48},{64,56},{72,6... | collective-permute-start | bytes 122888 | tf_op jit(solution)/shard_map/ppermute | solution.py:27
  574.0 7.0 %collective-permute-start.21 = (f32[5,16,10,1]{1,3,2,0:T(1,128)S(1)}, f32[5,16,10,1]{1,3,2,0:T(1,128)S(1)}, u32[]{:S(2)}, u32[]{:S(2)}) collective-permute-start(f32[5,16,10,1]{1,3,2,0:T(1,128)S(1)} %copy.125), channel_id=1, source_target_pairs={{0,1},{1,2},{2,3},{3,4},{4,5},{5,6},{6,7},{8,9},{9,10},{10,11},{11... | collective-permute-start | bytes 9608 | tf_op jit(solution)/shard_map/ppermute | solution.py:25
  578.1 15.7 %collective-permute-start.20 = (f32[5,16,10,1]{1,3,2,0:T(1,128)}, f32[5,16,10,1]{1,3,2,0:T(1,128)}, u32[]{:S(2)}, u32[]{:S(2)}) collective-permute-start(f32[5,16,10,1]{1,3,2,0:T(1,128)} %copy.123), channel_id=1, source_target_pairs={{1,0},{2,1},{3,2},{4,3},{5,4},{6,5},{7,6},{9,8},{10,9},{11,10},{12... | collective-permute-start | bytes 9608 | tf_op jit(solution)/shard_map/ppermute | solution.py:27
  598.1 5.9 collective-permute-start.23
  601.4 8.0 %collective-permute-start.22 = (f32[5,16,1,128]{3,0,2,1:T(8,128)S(1)}, f32[5,16,1,128]{3,0,2,1:T(8,128)S(1)}, u32[]{:S(2)}, u32[]{:S(2)}) collective-permute-start(f32[5,16,1,128]{3,0,2,1:T(8,128)S(1)} %get-tuple-element.71), channel_id=1, source_target_pairs={{8,0},{16,8},{24,16},{32,24},{40,32},{48,40},{56,48},{64,56},{72,6... | collective-permute-start | bytes 122888 | tf_op jit(solution)/shard_map/ppermute | solution.py:27
  610.7 7.1 %collective-permute-start.25 = (f32[5,16,10,1]{1,3,2,0:T(1,128)S(1)}, f32[5,16,10,1]{1,3,2,0:T(1,128)S(1)}, u32[]{:S(2)}, u32[]{:S(2)}) collective-permute-start(f32[5,16,10,1]{1,3,2,0:T(1,128)S(1)} %copy.129), channel_id=1, source_target_pairs={{0,1},{1,2},{2,3},{3,4},{4,5},{5,6},{6,7},{8,9},{9,10},{10,11},{11... | collective-permute-start | bytes 9608 | tf_op jit(solution)/shard_map/ppermute | solution.py:25
  613.6 15.7 %collective-permute-start.24 = (f32[5,16,10,1]{1,3,2,0:T(1,128)}, f32[5,16,10,1]{1,3,2,0:T(1,128)}, u32[]{:S(2)}, u32[]{:S(2)}) collective-permute-start(f32[5,16,10,1]{1,3,2,0:T(1,128)} %copy.127), channel_id=1, source_target_pairs={{1,0},{2,1},{3,2},{4,3},{5,4},{6,5},{7,6},{9,8},{10,9},{11,10},{12... | collective-permute-start | bytes 9608 | tf_op jit(solution)/shard_map/ppermute | solution.py:27
  (37 other events, 315.0 us)
where the time goes:
time: 643 us; the launch traced here: 633 us
  blocking collectives  341 us (53%)
  starting transfers between devices  132 us (21%)
  waiting for transfers between devices  62.9 us (10%)
  local copies, waits for them, and re-layouts  44.4 us (7%)
  matrix products  26.3 us (4%)
  other arithmetic  22.7 us (4%)
    psum x3, blocking collectives, per_device(): stiff_total = lax.psum(local_forces, 'chord')  341 us
    ppermute x9, waiting for transfers between devices, with_halo(): lax.ppermute(head, axis, [((i + 1) % count, i) for i in range(ends)])  60.6 us
    ppermute x8, starting transfers between devices, shifted(): lax.ppermute(value, axis, [(source, source + steps) for source in range(i...  60.6 us
    ppermute x9, starting transfers between devices, with_halo(): lax.ppermute(tail, axis, [(i, (i + 1) % count) for i in range(ends)])  52.4 us
    ppermute x9, starting transfers between devices, with_halo(): lax.ppermute(head, axis, [((i + 1) % count, i) for i in range(ends)])  19.4 us
    dot_general x12, matrix products, relax_cells(): jnp.einsum('ij,jnsc->insc', downwind[direction], backward, precision=lax....  13.2 us
  transfers between devices with their start and end apart: 26, of which 11 were waited for; matrix products, arithmetic and copies ran while one was open for 11% of the time, Pallas kernels for 0%

commit v1 on v0

--- a/solution.py
+++ b/solution.py
@@ -119,7 +119,7 @@
     shell_state = adjoint_shell
     for turn_index in range(SS):
         local_forces = element_terms(shell_state, element_stiffness, local_nodes)
-        stiff_total = lax.psum(local_forces, "chord")
+        stiff_total = jnp.sum(lax.all_gather(local_forces, "chord"), axis=0)
         residual = shell_grad - load_full - stiff_total
         shell_state = shell_state + jnp.einsum(
             "ijn,jn->in", node_precond, residual, precision=lax.Precision.HIGHEST

time: 643 us -> 510 us (0.79)
  the two profiles are of different devices: /device:TPU:223 before, /device:TPU:152 now
where the time goes in v1:
time: 510 us; the launch traced here: 500 us
  blocking collectives  257 us (50%)
  waiting for transfers between devices  87.5 us (17%)
  starting transfers between devices  79.9 us (16%)
  matrix products  28.3 us (6%)
  local copies, waits for them, and re-layouts  25.5 us (5%)
  other arithmetic  19.6 us (4%)
    all_gather x3, blocking collectives, per_device(): stiff_total = jnp.sum(lax.all_gather(local_forces, 'chord'), axis=0)  191 us
    psum x1, blocking collectives, per_device(): partial_value = lax.psum(partial_value, 'chord')  65.9 us
    ppermute x9, waiting for transfers between devices, with_halo(): lax.ppermute(head, axis, [((i + 1) % count, i) for i in range(ends)])  44.1 us
    ppermute x9, starting transfers between devices, with_halo(): lax.ppermute(tail, axis, [(i, (i + 1) % count) for i in range(ends)])  36.1 us
    ppermute x9, starting transfers between devices, with_halo(): lax.ppermute(head, axis, [((i + 1) % count, i) for i in range(ends)])  25.2 us
    ppermute x9, waiting for transfers between devices, with_halo(): lax.ppermute(tail, axis, [(i, (i + 1) % count) for i in range(ends)])  23.3 us
    ppermute x8, waiting for transfers between devices, shifted(): lax.ppermute(value, axis, [(source, source + steps) for source in range(i...  20.1 us
    ppermute x8, starting transfers between devices, shifted(): lax.ppermute(value, axis, [(source, source + steps) for source in range(i...  18.6 us
  transfers between devices with their start and end apart: 26, of which 12 were waited for; matrix products, arithmetic and copies ran while one was open for 11% of the time, Pallas kernels for 0%

profile of v1, /device:TPU:152, one launch (start us, length us, event | category | flops | bytes accessed | tf_op | source)
XLA Modules:
  0.0 500.1 jit_solution(6169982924030445527)
XLA Ops:
  1.3 3.6 collective-permute-start.2
  8.9 6.4 %scatter_custom_fusion = f32[3072,3]{1,0:T(8,128)S(1)} fusion(s32[1024]{0:T(1024)S(1)} %subtract_bitcast_fusion.3, f32[1024,3]{1,0:T(8,128)S(1)} %bitcast.209, f32[]{:T(128)} %constant.118.clone.1), kind=kCustom, calls=%fused_computation.52 | custom fusion | flops 3072 | bytes 36868 | tf_op jit(solution)/shard_map/scatter-add | solution.py:112
  15.8 65.9 %psum.7 = f32[3,3072]{1,0:T(4,128)S(1)} all-reduce(f32[3,3072]{1,0:T(4,128)S(1)} %bitcast.213), channel_id=1, replica_groups=mesh['span'=64,'chord'=8] {'chord'}, use_global_device_ids=true, to_apply=%region_1.0 | all-reduce | flops 9216 | bytes 73728 | tf_op jit(solution)/shard_map/psum | solution.py:115
  84.2 2.4 collective-permute-start
  89.5 7.0 %collective-permute-start.10 = (f32[5,16,1,128]{3,0,2,1:T(8,128)}, f32[5,16,1,128]{3,0,2,1:T(8,128)}, u32[]{:S(2)}, u32[]{:S(2)}) collective-permute-start(f32[5,16,1,128]{3,0,2,1:T(8,128)} %get-tuple-element.76), channel_id=1, source_target_pairs={{8,0},{16,8},{24,16},{32,24},{40,32},{48,40},{56,48},{64,56},{72,6... | collective-permute-start | bytes 122888 | tf_op jit(solution)/shard_map/ppermute | solution.py:27
  104.6 6.6 %collective-permute-done.3 = f32[6,64]{0,1:T(8,128)S(1)} collective-permute-done((f32[6,64]{0,1:T(8,128)S(1)}, f32[6,64]{0,1:T(8,128)S(1)}, u32[]{:S(2)}, u32[]{:S(2)}) %collective-permute-start.3) | collective-permute-done | bytes 1568 | tf_op jit(solution)/shard_map/ppermute | solution.py:14
  112.0 63.6 %all_gather.26 = f32[8,6,1024]{2,1,0:T(8,128)S(1)} all-gather(f32[1,6,1024]{2,1,0:T(8,128)S(1)} %copy.190), channel_id=1, replica_groups=mesh['span'=64,'chord'=8] {'chord'}, dimensions={0}, use_global_device_ids=true | all-gather | bytes 221184 | tf_op jit(solution)/shard_map/all_gather | solution.py:122
  182.4 2.5 scatter_custom_fusion.2
  184.9 2.4 collective-permute-start.5
  187.3 6.1 %collective-permute-done.5 = f32[6,64]{0,1:T(8,128)S(1)} collective-permute-done((f32[6,64]{0,1:T(8,128)S(1)}, f32[6,64]{0,1:T(8,128)S(1)}, u32[]{:S(2)}, u32[]{:S(2)}) %collective-permute-start.5) | collective-permute-done | bytes 1568 | tf_op jit(solution)/shard_map/ppermute | solution.py:14
  194.3 63.3 %all_gather.29 = f32[8,6,1024]{2,1,0:T(8,128)S(1)} all-gather(f32[1,6,1024]{2,1,0:T(8,128)S(1)} %copy.194), channel_id=1, replica_groups=mesh['span'=64,'chord'=8] {'chord'}, dimensions={0}, use_global_device_ids=true | all-gather | bytes 221184 | tf_op jit(solution)/shard_map/all_gather | solution.py:122
  262.6 2.5 scatter_custom_fusion.3
  267.3 6.6 %collective-permute-done.7 = f32[6,64]{0,1:T(8,128)S(1)} collective-permute-done((f32[6,64]{0,1:T(8,128)S(1)}, f32[6,64]{0,1:T(8,128)S(1)}, u32[]{:S(2)}, u32[]{:S(2)}) %collective-permute-start.7) | collective-permute-done | bytes 1568 | tf_op jit(solution)/shard_map/ppermute | solution.py:14
  274.7 63.7 %all_gather.32 = f32[8,6,1024]{2,1,0:T(8,128)S(1)} all-gather(f32[1,6,1024]{2,1,0:T(8,128)S(1)} %copy.198), channel_id=1, replica_groups=mesh['span'=64,'chord'=8] {'chord'}, dimensions={0}, use_global_device_ids=true | all-gather | bytes 221184 | tf_op jit(solution)/shard_map/all_gather | solution.py:122
  340.5 2.4 collective-permute-start.8
  343.2 5.7 %collective-permute-done.8 = f32[3,1024]{1,0:T(4,128)S(1)} collective-permute-done((f32[3,1024]{1,0:T(4,128)S(1)}, f32[3,1024]{1,0:T(4,128)S(1)}, u32[]{:S(2)}, u32[]{:S(2)}) %collective-permute-start.8) | collective-permute-done | bytes 12320 | tf_op jit(solution)/shard_map/ppermute | solution.py:25
  349.4 4.0 gather_fusion.3
  357.3 15.0 %collective-permute-start.13 = (f32[5,16,10,1]{1,3,2,0:T(1,128)S(1)}, f32[5,16,10,1]{1,3,2,0:T(1,128)S(1)}, u32[]{:S(2)}, u32[]{:S(2)}) collective-permute-start(f32[5,16,10,1]{1,3,2,0:T(1,128)S(1)} %copy.214), channel_id=1, source_target_pairs={{0,1},{1,2},{2,3},{3,4},{4,5},{5,6},{6,7},{8,9},{9,10},{10,11},{11... | collective-permute-start | bytes 9608 | tf_op jit(solution)/shard_map/ppermute | solution.py:25
  378.7 10.5 %collective-permute-done.12 = f32[5,16,10,1]{1,3,2,0:T(1,128)S(1)} collective-permute-done((f32[5,16,10,1]{1,3,2,0:T(1,128)S(1)}, f32[5,16,10,1]{1,3,2,0:T(1,128)S(1)}, u32[]{:S(2)}, u32[]{:S(2)}) %collective-permute-start.12) | collective-permute-done | bytes 3232 | tf_op jit(solution)/shard_map/ppermute | solution.py:27
  395.9 2.4 collective-permute-start.15
  398.9 5.9 %collective-permute-done.15 = f32[5,16,1,128]{3,0,2,1:T(8,128)S(1)} collective-permute-done((f32[5,16,1,128]{3,0,2,1:T(8,128)S(1)}, f32[5,16,1,128]{3,0,2,1:T(8,128)S(1)}, u32[]{:S(2)}, u32[]{:S(2)}) %collective-permute-start.15) | collective-permute-done | bytes 40992 | tf_op jit(solution)/shard_map/ppermute | solution.py:25
  405.5 4.3 collective-permute-start.17
  414.7 12.0 %collective-permute-done.16 = f32[5,16,10,1]{1,3,2,0:T(1,128)S(1)} collective-permute-done((f32[5,16,10,1]{1,3,2,0:T(1,128)S(1)}, f32[5,16,10,1]{1,3,2,0:T(1,128)S(1)}, u32[]{:S(2)}, u32[]{:S(2)}) %collective-permute-start.16) | collective-permute-done | bytes 3232 | tf_op jit(solution)/shard_map/ppermute | solution.py:27
  432.2 2.4 collective-permute-start.19
  435.2 5.9 %collective-permute-done.19 = f32[5,16,1,128]{3,0,2,1:T(8,128)S(1)} collective-permute-done((f32[5,16,1,128]{3,0,2,1:T(8,128)S(1)}, f32[5,16,1,128]{3,0,2,1:T(8,128)S(1)}, u32[]{:S(2)}, u32[]{:S(2)}) %collective-permute-start.19) | collective-permute-done | bytes 40992 | tf_op jit(solution)/shard_map/ppermute | solution.py:25
  441.8 2.8 collective-permute-start.21
  444.9 3.1 collective-permute-start.20
  450.5 11.0 %collective-permute-done.20 = f32[5,16,10,1]{1,3,2,0:T(1,128)S(1)} collective-permute-done((f32[5,16,10,1]{1,3,2,0:T(1,128)S(1)}, f32[5,16,10,1]{1,3,2,0:T(1,128)S(1)}, u32[]{:S(2)}, u32[]{:S(2)}) %collective-permute-start.20) | collective-permute-done | bytes 3232 | tf_op jit(solution)/shard_map/ppermute | solution.py:27
  470.0 5.9 %collective-permute-done.23 = f32[5,16,1,128]{3,0,2,1:T(8,128)S(1)} collective-permute-done((f32[5,16,1,128]{3,0,2,1:T(8,128)S(1)}, f32[5,16,1,128]{3,0,2,1:T(8,128)S(1)}, u32[]{:S(2)}, u32[]{:S(2)}) %collective-permute-start.23) | collective-permute-done | bytes 40992 | tf_op jit(solution)/shard_map/ppermute | solution.py:25
  476.5 2.6 collective-permute-start.25
  479.5 3.5 collective-permute-start.24
  485.5 10.6 %collective-permute-done.24 = f32[5,16,10,1]{1,3,2,0:T(1,128)S(1)} collective-permute-done((f32[5,16,10,1]{1,3,2,0:T(1,128)S(1)}, f32[5,16,10,1]{1,3,2,0:T(1,128)S(1)}, u32[]{:S(2)}, u32[]{:S(2)}) %collective-permute-start.24) | collective-permute-done | bytes 3232 | tf_op jit(solution)/shard_map/ppermute | solution.py:27
  (215 shorter events, 85.0 us)
Async XLA Ops:
  1.3 97.2 %collective-permute-start.2 = (f32[6,64]{1,0:T(8,128)S(1)}, f32[6,64]{1,0:T(8,128)S(1)}, u32[]{:S(2)}, u32[]{:S(2)}) collective-permute-start(f32[6,64]{1,0:T(8,128)S(1)} %slice.324), channel_id=1, source_target_pairs={{8,0},{16,8},{24,16},{32,24},{40,32},{48,40},{56,48},{64,56},{72,6... | collective-permute-start | bytes 4616 | tf_op jit(solution)/shard_map/ppermute | solution.py:14
  15.3 81.1 %copy-start.19 = (f32[3,5,5]{2,0,1:T(4,128)S(1)}, f32[3,5,5]{2,0,1:T(4,128)}, u32[]{:S(2)}) copy-start(f32[3,5,5]{2,0,1:T(4,128)} %param.28) | copy-start | bytes 904
  15.3 81.7 %copy-start.8 = (f32[3,16,8,128]{3,2,1,0:T(8,128)S(1)}, f32[3,16,8,128]{3,2,1,0:T(8,128)}, u32[]{:S(2)}) copy-start(f32[3,16,8,128]{3,2,1,0:T(8,128)} %param.26) | copy-start | bytes 589828
  15.4 81.7 %copy-start.20 = (f32[3,5,5]{2,0,1:T(4,128)S(1)}, f32[3,5,5]{2,0,1:T(4,128)}, u32[]{:S(2)}) copy-start(f32[3,5,5]{2,0,1:T(4,128)} %param.27) | copy-start | bytes 904
  15.8 81.9 %copy-start.23 = (s32[4,128]{1,0:T(4,128)S(1)}, s32[4,128]{1,0:T(4,128)}, u32[]{:S(2)}) copy-start(s32[4,128]{1,0:T(4,128)} %param.37) | copy-start | bytes 6148
  15.8 82.7 %copy-start.9 = (f32[6,1024]{1,0:T(8,128)S(1)}, f32[6,1024]{1,0:T(8,128)}, u32[]{:S(2)}) copy-start(f32[6,1024]{1,0:T(8,128)} %param.33) | copy-start | bytes 73732
  82.3 93.3 %collective-permute-start.1 = (f32[3,1024]{1,0:T(4,128)}, f32[3,1024]{1,0:T(4,128)}, u32[]{:S(2)}, u32[]{:S(2)}) collective-permute-start(f32[3,1024]{1,0:T(4,128)} %get-tuple-element.82), channel_id=1, source_target_pairs={{8,0},{16,8},{24,16},{32,24},{40,32},{48,40},{56,48},{64,56},{72,6... | collective-permute-start | bytes 36872 | tf_op jit(solution)/shard_map/ppermute | solution.py:14
  84.2 91.4 %collective-permute-start = (f32[3,1024]{1,0:T(4,128)}, f32[3,1024]{1,0:T(4,128)}, u32[]{:S(2)}, u32[]{:S(2)}) collective-permute-start(f32[3,1024]{1,0:T(4,128)} %get-tuple-element.81), channel_id=1, source_target_pairs={{0,8},{8,16},{16,24},{24,32},{32,40},{40,48},{48,56},{56,64},{64,7... | collective-permute-start | bytes 36872 | tf_op jit(solution)/shard_map/ppermute | solution.py:14
  87.5 267.3 %collective-permute-start.11 = (f32[5,16,1,128]{3,0,2,1:T(8,128)}, f32[5,16,1,128]{3,0,2,1:T(8,128)}, u32[]{:S(2)}, u32[]{:S(2)}) collective-permute-start(f32[5,16,1,128]{3,0,2,1:T(8,128)} %get-tuple-element.77), channel_id=1, source_target_pairs={{0,8},{8,16},{16,24},{24,32},{32,40},{40,48},{48,56},{56,64},{64,7... | collective-permute-start | bytes 122888 | tf_op jit(solution)/shard_map/ppermute | solution.py:25
  89.5 266.4 %collective-permute-start.10 = (f32[5,16,1,128]{3,0,2,1:T(8,128)}, f32[5,16,1,128]{3,0,2,1:T(8,128)}, u32[]{:S(2)}, u32[]{:S(2)}) collective-permute-start(f32[5,16,1,128]{3,0,2,1:T(8,128)} %get-tuple-element.76), channel_id=1, source_target_pairs={{8,0},{16,8},{24,16},{32,24},{40,32},{48,40},{56,48},{64,56},{72,6... | collective-permute-start | bytes 122888 | tf_op jit(solution)/shard_map/ppermute | solution.py:27
  97.1 81.4 %copy-start.4 = (f32[16,8,128]{2,1,0:T(8,128)}, f32[16,8,128]{2,1,0:T(8,128)S(1)}, u32[]{:S(2)}) copy-start(f32[16,8,128]{2,1,0:T(8,128)S(1)} %get-tuple-element.79) | copy-start | bytes 196612
  102.6 8.6 %collective-permute-start.3 = (f32[6,64]{0,1:T(8,128)S(1)}, f32[6,64]{0,1:T(8,128)S(1)}, u32[]{:S(2)}, u32[]{:S(2)}) collective-permute-start(f32[6,64]{0,1:T(8,128)S(1)} %slice.400), channel_id=1, source_target_pairs={{0,8},{8,16},{16,24},{24,32},{32,40},{40,48},{48,56},{56,64},{64,7... | collective-permute-start | bytes 4616 | tf_op jit(solution)/shard_map/ppermute | solution.py:14
  176.5 4.2 collective-permute-start.4
  184.9 8.6 %collective-permute-start.5 = (f32[6,64]{0,1:T(8,128)S(1)}, f32[6,64]{0,1:T(8,128)S(1)}, u32[]{:S(2)}, u32[]{:S(2)}) collective-permute-start(f32[6,64]{0,1:T(8,128)S(1)} %slice.404), channel_id=1, source_target_pairs={{0,8},{8,16},{16,24},{24,32},{32,40},{40,48},{48,56},{56,64},{64,7... | collective-permute-start | bytes 4616 | tf_op jit(solution)/shard_map/ppermute | solution.py:14
  257.7 3.2 collective-permute-start.6
  265.2 8.7 %collective-permute-start.7 = (f32[6,64]{0,1:T(8,128)S(1)}, f32[6,64]{0,1:T(8,128)S(1)}, u32[]{:S(2)}, u32[]{:S(2)}) collective-permute-start(f32[6,64]{0,1:T(8,128)S(1)} %slice.408), channel_id=1, source_target_pairs={{0,8},{8,16},{16,24},{24,32},{32,40},{40,48},{48,56},{56,64},{64,7... | collective-permute-start | bytes 4616 | tf_op jit(solution)/shard_map/ppermute | solution.py:14
  338.5 4.6 collective-permute-start.9
  340.5 8.4 %collective-permute-start.8 = (f32[3,1024]{1,0:T(4,128)S(1)}, f32[3,1024]{1,0:T(4,128)S(1)}, u32[]{:S(2)}, u32[]{:S(2)}) collective-permute-start(f32[3,1024]{1,0:T(4,128)S(1)} %slice.409), channel_id=1, source_target_pairs={{0,8},{8,16},{16,24},{24,32},{32,40},{40,48},{48,56},{56,64},{64,7... | collective-permute-start | bytes 36872 | tf_op jit(solution)/shard_map/ppermute | solution.py:25
  357.3 19.5 %collective-permute-start.13 = (f32[5,16,10,1]{1,3,2,0:T(1,128)S(1)}, f32[5,16,10,1]{1,3,2,0:T(1,128)S(1)}, u32[]{:S(2)}, u32[]{:S(2)}) collective-permute-start(f32[5,16,10,1]{1,3,2,0:T(1,128)S(1)} %copy.214), channel_id=1, source_target_pairs={{0,1},{1,2},{2,3},{3,4},{4,5},{5,6},{6,7},{8,9},{9,10},{10,11},{11... | collective-permute-start | bytes 9608 | tf_op jit(solution)/shard_map/ppermute | solution.py:25
  372.7 16.5 %collective-permute-start.12 = (f32[5,16,10,1]{1,3,2,0:T(1,128)S(1)}, f32[5,16,10,1]{1,3,2,0:T(1,128)S(1)}, u32[]{:S(2)}, u32[]{:S(2)}) collective-permute-start(f32[5,16,10,1]{1,3,2,0:T(1,128)S(1)} %copy.211), channel_id=1, source_target_pairs={{1,0},{2,1},{3,2},{4,3},{5,4},{6,5},{7,6},{9,8},{10,9},{11,10},{12... | collective-permute-start | bytes 9608 | tf_op jit(solution)/shard_map/ppermute | solution.py:27
  394.0 5.0 collective-permute-start.14
  395.9 8.9 %collective-permute-start.15 = (f32[5,16,1,128]{3,0,2,1:T(8,128)S(1)}, f32[5,16,1,128]{3,0,2,1:T(8,128)S(1)}, u32[]{:S(2)}, u32[]{:S(2)}) collective-permute-start(f32[5,16,1,128]{3,0,2,1:T(8,128)S(1)} %get-tuple-element.74), channel_id=1, source_target_pairs={{0,8},{8,16},{16,24},{24,32},{32,40},{40,48},{48,56},{56,64},{64,7... | collective-permute-start | bytes 122888 | tf_op jit(solution)/shard_map/ppermute | solution.py:25
  405.5 8.1 %collective-permute-start.17 = (f32[5,16,10,1]{1,3,2,0:T(1,128)S(1)}, f32[5,16,10,1]{1,3,2,0:T(1,128)S(1)}, u32[]{:S(2)}, u32[]{:S(2)}) collective-permute-start(f32[5,16,10,1]{1,3,2,0:T(1,128)S(1)} %copy.219), channel_id=1, source_target_pairs={{0,1},{1,2},{2,3},{3,4},{4,5},{5,6},{6,7},{8,9},{9,10},{10,11},{11... | collective-permute-start | bytes 9608 | tf_op jit(solution)/shard_map/ppermute | solution.py:25
  410.1 16.5 %collective-permute-start.16 = (f32[5,16,10,1]{1,3,2,0:T(1,128)S(1)}, f32[5,16,10,1]{1,3,2,0:T(1,128)S(1)}, u32[]{:S(2)}, u32[]{:S(2)}) collective-permute-start(f32[5,16,10,1]{1,3,2,0:T(1,128)S(1)} %copy.217), channel_id=1, source_target_pairs={{1,0},{2,1},{3,2},{4,3},{5,4},{6,5},{7,6},{9,8},{10,9},{11,10},{12... | collective-permute-start | bytes 9608 | tf_op jit(solution)/shard_map/ppermute | solution.py:27
  430.2 4.9 collective-permute-start.18
  432.2 8.9 %collective-permute-start.19 = (f32[5,16,1,128]{3,0,2,1:T(8,128)S(1)}, f32[5,16,1,128]{3,0,2,1:T(8,128)S(1)}, u32[]{:S(2)}, u32[]{:S(2)}) collective-permute-start(f32[5,16,1,128]{3,0,2,1:T(8,128)S(1)} %get-tuple-element.72), channel_id=1, source_target_pairs={{0,8},{8,16},{16,24},{24,32},{32,40},{40,48},{48,56},{56,64},{64,7... | collective-permute-start | bytes 122888 | tf_op jit(solution)/shard_map/ppermute | solution.py:25
  441.8 7.6 %collective-permute-start.21 = (f32[5,16,10,1]{1,3,2,0:T(1,128)S(1)}, f32[5,16,10,1]{1,3,2,0:T(1,128)S(1)}, u32[]{:S(2)}, u32[]{:S(2)}) collective-permute-start(f32[5,16,10,1]{1,3,2,0:T(1,128)S(1)} %copy.223), channel_id=1, source_target_pairs={{0,1},{1,2},{2,3},{3,4},{4,5},{5,6},{6,7},{8,9},{9,10},{10,11},{11... | collective-permute-start | bytes 9608 | tf_op jit(solution)/shard_map/ppermute | solution.py:25
  444.9 16.5 %collective-permute-start.20 = (f32[5,16,10,1]{1,3,2,0:T(1,128)S(1)}, f32[5,16,10,1]{1,3,2,0:T(1,128)S(1)}, u32[]{:S(2)}, u32[]{:S(2)}) collective-permute-start(f32[5,16,10,1]{1,3,2,0:T(1,128)S(1)} %copy.221), channel_id=1, source_target_pairs={{1,0},{2,1},{3,2},{4,3},{5,4},{6,5},{7,6},{9,8},{10,9},{11,10},{12... | collective-permute-start | bytes 9608 | tf_op jit(solution)/shard_map/ppermute | solution.py:27
  465.0 4.9 collective-permute-start.22
  467.0 8.9 %collective-permute-start.23 = (f32[5,16,1,128]{3,0,2,1:T(8,128)S(1)}, f32[5,16,1,128]{3,0,2,1:T(8,128)S(1)}, u32[]{:S(2)}, u32[]{:S(2)}) collective-permute-start(f32[5,16,1,128]{3,0,2,1:T(8,128)S(1)} %get-tuple-element.70), channel_id=1, source_target_pairs={{0,8},{8,16},{16,24},{24,32},{32,40},{40,48},{48,56},{56,64},{64,7... | collective-permute-start | bytes 122888 | tf_op jit(solution)/shard_map/ppermute | solution.py:25
  476.5 7.8 %collective-permute-start.25 = (f32[5,16,10,1]{1,3,2,0:T(1,128)S(1)}, f32[5,16,10,1]{1,3,2,0:T(1,128)S(1)}, u32[]{:S(2)}, u32[]{:S(2)}) collective-permute-start(f32[5,16,10,1]{1,3,2,0:T(1,128)S(1)} %copy.227), channel_id=1, source_target_pairs={{0,1},{1,2},{2,3},{3,4},{4,5},{5,6},{6,7},{8,9},{9,10},{10,11},{11... | collective-permute-start | bytes 9608 | tf_op jit(solution)/shard_map/ppermute | solution.py:25
  479.5 16.5 %collective-permute-start.24 = (f32[5,16,10,1]{1,3,2,0:T(1,128)S(1)}, f32[5,16,10,1]{1,3,2,0:T(1,128)S(1)}, u32[]{:S(2)}, u32[]{:S(2)}) collective-permute-start(f32[5,16,10,1]{1,3,2,0:T(1,128)S(1)} %copy.225), channel_id=1, source_target_pairs={{1,0},{2,1},{3,2},{4,3},{5,4},{6,5},{7,6},{9,8},{10,9},{11,10},{12... | collective-permute-start | bytes 9608 | tf_op jit(solution)/shard_map/ppermute | solution.py:27
  (20 other events, 638.1 us)
